TPU v7x, 32 devices: a whole 2x2x4 slice. The times are simulated.
32 devices in a mesh: grp: 4 (over z), dev: 8 (over y, x, core).
Axes of the slice: x: 2, y: 2, z: 4, core: 2. Of those that a mesh axis runs over, the one named last changes fastest.
Arguments:
- vertex_values: bfloat16 [2048, 128, 256], P(('grp', 'dev')), may hold values from -6 to 6
- position_domain_label: int32 [2048], P(('grp', 'dev')), may hold values from 0 to 64, as said below
- position_vertex_tally: int32 [2048], P(('grp', 'dev')), may hold values from 0 to 128, as said below
- normalizer_gain: float32 [256], replicated, may hold values from 0.1 to 1.9
- embedding_matrix: bfloat16 [256, 256], replicated, may hold values from -0.375 to 0.375
- partition_input_matrix: bfloat16 [256, 256], replicated, may hold values from -0.375 to 0.375
- partition_score_matrix: bfloat16 [32, 64], replicated, may hold values from -60 to 60
- softmax_sharpness: float32 [8], replicated, may hold values from 0.3 to 1
- partition_attention_maps: float32 [3, 32, 32], replicated, may hold values from -10 to 10
- readout_matrix: bfloat16 [256, 256], replicated, may hold values from -1.5 to 1.5
Outputs:
- updated: bfloat16 [2048, 128, 256], P(('grp', 'dev'))
Inputs may be any that keep to these rules, and one draw needn't show every extreme that they name: `position_domain_label`: on each device the used slots come first; a device may use none. Reading the devices in order and their used slots in order lists every mesh's blocks as one run, meshes in increasing order, each mesh 2 or more blocks. Exactly 1024 slots are used in all, and some device uses all 64 of its slots. `position_vertex_tally`: 128 in every used slot except the last block of each mesh, which holds 1 to 128; 0 in unused slots.
All inputs are finite; a program needn't handle non-finite values.
Results may differ from a plain program's by a relative error of at most 0.012.
The roundings to bfloat16 on the way count: a program that leaves them out, or rounds other values in their place, can miss the bound.
Values may be sent and summed in bfloat16 or wider, within the bound.
A program may use at most 128 MiB of HBM per device.

v0:
```python
import functools
import math

import jax
import jax.numpy as jnp
from jax import lax
from jax.experimental import pallas as pl
from jax.experimental.pallas import tpu as pltpu
from jax.sharding import PartitionSpec as P

MESHES = 64
CHUNK = 4
MESH_ID = pl.DeviceIdType.MESH
NT = (((1,), (1,)), ((), ()))
F32 = jnp.float32
BF16 = jnp.bfloat16
LOG2E = math.log2(math.e)


def dot(a, b):
    return jnp.dot(a, b, preferred_element_type=F32)


def dot_nt(a, b):
    return lax.dot_general(a, b, NT, preferred_element_type=F32)


def halves(x):
    high = x.astype(BF16)
    return high, (x - high.astype(F32)).astype(BF16)


def dot3(a, b, product=dot):
    return product(a[0], b[0]) + (product(a[0], b[1]) + product(a[1], b[0]))


def lanes(shape):
    return lax.broadcasted_iota(jnp.int32, shape, len(shape) - 1)


def tiler(dim, width):
    row = lax.broadcasted_iota(jnp.int32, (dim, width), 0)
    return (row == lanes((dim, width)) % dim).astype(BF16)


def gather_kernel(
    heads,
    label_ref,
    tally_ref,
    x_ref,
    gain_ref,
    embed_ref,
    inputs_ref,
    score_ref,
    sharp_ref,
    shares_ref,
    sums_ref,
    ends_ref,
    end_ref,
    running_ref,
    inputs_t_ref,
    score_t_ref,
):
    step = pl.program_id(0)
    chunk, height, width = x_ref.shape
    points = chunk * height
    dim, parts = score_ref.shape
    half = width // 2
    group = heads // 2
    slots = label_ref.shape[0]

    @pl.when(step == 0)
    def _():
        running_ref[...] = jnp.zeros_like(running_ref)
        ends_ref[...] = jnp.zeros_like(ends_ref)
        inputs_t_ref[...] = inputs_ref[...].T
        tiled = lax.dot_general(
            score_ref[...],
            tiler(dim, width),
            (((0,), (0,)), ((), ())),
            preferred_element_type=F32,
        )
        lane = lanes((parts, width)) // dim
        for h in range(heads):
            score_t_ref[h * parts : (h + 1) * parts] = jnp.where(
                lane == h, tiled, 0.0
            ).astype(BF16)

        def note(i, carry):
            follower, last, order = carry
            k = slots - 1 - i
            here = label_ref[k]
            differs = here != label_ref[jnp.minimum(k + 1, slots - 1)]
            follower = jnp.where(differs, k, follower)
            order = order + differs.astype(jnp.int32)
            end_ref[k] = follower
            end_ref[slots + k] = order % chunk
            return follower, jnp.maximum(last, jnp.where(here < MESHES, here, -1)), order

        end_ref[2 * slots] = lax.fori_loop(
            0, slots, note, (jnp.int32(slots - 1), jnp.int32(-1), jnp.int32(0))
        )[1]

    x = x_ref[...].reshape(points, width).astype(F32)
    centre = x - jnp.mean(x, axis=1, keepdims=True)
    var = jnp.mean(centre * centre, axis=1, keepdims=True)
    normed = (centre * lax.rsqrt(var + 1e-05) * gain_ref[...]).astype(BF16)
    features = dot(normed, embed_ref[...]).astype(BF16)
    middles = dot_nt(inputs_t_ref[...], normed).astype(BF16)
    lane = lanes((1, height))
    living = jnp.concatenate(
        [
            (lane < tally_ref[step * chunk + b]).astype(F32)
            for b in range(chunk)
        ],
        axis=1,
    )
    for h in range(heads):
        rows = dot(
            score_t_ref[h * parts : (h + 1) * parts, h // group * half : (h // group + 1) * half],
            middles[h // group * half : (h // group + 1) * half],
        )
        top = jnp.max(rows, axis=0, keepdims=True)
        sharp = LOG2E / jnp.full((1, points), sharp_ref[h], F32)
        powers = jnp.exp2((rows - top) * sharp)
        scale = living / jnp.sum(powers, axis=0, keepdims=True)
        shares_ref[0, h * parts : (h + 1) * parts, :] = (powers * scale).astype(BF16)

    ones = jnp.ones((height, 128), BF16)
    share_lane = lanes((parts, half)) // dim
    total_lane = lanes((parts, 128))
    running = running_ref[...]
    for b in range(chunk):
        slot = step * chunk + b
        same = label_ref[slot] == label_ref[jnp.maximum(slot - 1, 0)]
        pieces = []
        totals = None
        for g in range(2):
            right = jnp.concatenate(
                [
                    features[b * height : (b + 1) * height, g * half : (g + 1) * half],
                    ones,
                ],
                axis=1,
            )
            got = dot(
                shares_ref[
                    0,
                    g * group * parts : (g + 1) * group * parts,
                    b * height : (b + 1) * height,
                ],
                right,
            )
            piece = got[:parts, :half]
            for i in range(group):
                mine = got[i * parts : (i + 1) * parts]
                piece = jnp.where(share_lane == i, mine[:, :half], piece)
                if totals is None:
                    totals = mine[:, half:]
                else:
                    totals = jnp.where(
                        total_lane == g * group + i, mine[:, half:], totals
                    )
            pieces.append(piece)
        running = jnp.where(same, running, 0.0) + jnp.concatenate(
            pieces + [totals], axis=1
        )
        sums_ref[b] = running
    running_ref[...] = running
    for b in range(chunk):
        slot = step * chunk + b
        label = label_ref[slot]
        stop = jnp.logical_and(label < MESHES, end_ref[slot] == slot)

        @pl.when(jnp.logical_and(stop, label == label_ref[0]))
        def _():
            ends_ref[0] = sums_ref[b]

        @pl.when(jnp.logical_and(stop, label == end_ref[2 * slots]))
        def _():
            ends_ref[1] = sums_ref[b]


def exchange_kernel(
    axes, heads, label_ref, end_ref, ends_ref, out_ref, held, sent, send_sem, recv_sem
):
    parts = out_ref.shape[1]
    width = out_ref.shape[2] - 128
    partners = []
    for name, size in reversed(axes):
        bit = 1
        while bit < size:
            at = {n: lax.axis_index(n) for n, _ in axes}
            here = at[name]
            at[name] = here + bit - 2 * bit * (here // bit % 2)
            partners.append(tuple(at[n] for n, _ in axes))
            bit *= 2
    barrier = pltpu.get_barrier_semaphore()
    for partner in partners:
        pl.semaphore_signal(barrier, inc=1, device_id=partner, device_id_type=MESH_ID)

    def own(i):
        totals = ends_ref[i, :, width:].T[:heads]
        totals = jnp.concatenate([totals, jnp.zeros((heads, width - parts), F32)], axis=1)
        full = jnp.concatenate([ends_ref[i, :, :width], totals], axis=0)
        return full.reshape(-1, 8, width)

    def put(i, k, values, ids):
        sent[i, k] = jnp.concatenate([values.reshape(-1, width), ids], axis=0).astype(BF16)

    def load(i, k):
        block = held[i, k].astype(F32)
        return block[: parts + heads].reshape(-1, 8, width), block[parts + heads :]

    first = group_first = own(0)
    last = group_last = own(1)
    ids = (8, width)
    first_id = group_first_id = jnp.full(ids, label_ref[0].astype(F32), F32)
    last_id = group_last_id = jnp.full(
        ids, end_ref[end_ref.shape[0] - 1].astype(F32), F32
    )
    put(0, 0, first, first_id)
    put(0, 1, last, last_id)
    pl.semaphore_wait(barrier, len(partners))
    for i, partner in enumerate(partners):
        copy = pltpu.make_async_remote_copy(
            src_ref=sent.at[i],
            dst_ref=held.at[i],
            send_sem=send_sem.at[i],
            recv_sem=recv_sem.at[i],
            device_id=partner,
            device_id_type=MESH_ID,
        )
        copy.start()
        copy.wait()
        other_first, other_first_id = load(i, 0)
        other_last, other_last_id = load(i, 1)
        if i < len(partners) - 1:
            new_first_id = jnp.minimum(group_first_id, other_first_id)
            new_last_id = jnp.maximum(group_last_id, other_last_id)
            group_first = jnp.where(
                (group_first_id == new_first_id)[None], group_first, 0.0
            ) + jnp.where((other_first_id == new_first_id)[None], other_first, 0.0)
            group_last = jnp.where(
                (group_last_id == new_last_id)[None], group_last, 0.0
            ) + jnp.where((other_last_id == new_last_id)[None], other_last, 0.0)
            group_first_id, group_last_id = new_first_id, new_last_id
            put(i + 1, 0, group_first, group_first_id)
            put(i + 1, 1, group_last, group_last_id)

    def found(i, own_id):
        other_first, other_first_id = load(i, 0)
        other_last, other_last_id = load(i, 1)
        return jnp.where(
            (own_id == other_first_id)[None],
            other_first,
            jnp.where((own_id == other_last_id)[None], other_last, 0.0),
        )

    for k, (total, own_id) in enumerate([(first, first_id), (last, last_id)]):
        for i in range(len(partners)):
            total = total + found(i, own_id)
        total = total.reshape(-1, width)
        rows = jnp.concatenate(
            [total[parts:, :128], jnp.zeros((128 - heads, 128), F32)], axis=0
        )
        out_ref[k] = jnp.concatenate([total[:parts], rows.T[:parts]], axis=1)


def spread_kernel(
    heads,
    label_ref,
    tally_ref,
    end_ref,
    x_ref,
    shares_ref,
    *refs,
):
    chunk, height, width = x_ref.shape
    sums_refs = refs[:chunk]
    ends_ref, maps_ref, readout_ref, out_ref, mixed_ref, map_ref = refs[chunk:]
    step = pl.program_id(0)
    parts = ends_ref.shape[1]
    dim = width // heads
    slots = label_ref.shape[0]
    last_label = end_ref[end_ref.shape[0] - 1]

    @pl.when(step == 0)
    def _():
        across = tiler(dim, width)
        row = lax.broadcasted_iota(jnp.int32, (width, dim), 0)
        down = (row % dim == lanes((width, dim))).astype(BF16)
        same = (
            lax.broadcasted_iota(jnp.int32, (width, width), 0) // dim
            == lanes((width, width)) // dim
        )
        for i in range(3):
            for j, part in enumerate(halves(maps_ref[i])):
                tall = dot(down, part) if i < 2 else dot_nt(down, part)
                map_ref[i, j] = jnp.where(same, dot(tall.astype(BF16), across), 0.0).astype(BF16)

    for b in range(chunk):
        slot = step * chunk + b
        label = label_ref[slot]
        fresh = jnp.logical_or(slot == 0, label != label_ref[jnp.maximum(slot - 1, 0)])

        @pl.when(jnp.logical_and(fresh, label < MESHES))
        def _():
            is_first = label == label_ref[0]
            is_last = label == last_label
            state = jnp.where(
                is_first,
                ends_ref[0],
                jnp.where(is_last, ends_ref[1], sums_refs[b][0]),
            )
            high, low = halves(state[:, width:])
            expand = (
                lax.broadcasted_iota(jnp.int32, (128, width), 0)
                == lanes((128, width)) // dim
            ).astype(BF16)
            totals = dot(high, expand) + dot(low, expand)
            tokens = state[:, :width] / (totals + 1.0)
            tokens = jnp.concatenate([tokens, tokens], axis=0)
            split = halves(tokens)
            maps = [(map_ref[i, 0], map_ref[i, 1]) for i in range(3)]
            queries = halves(dot3(split, maps[0]))
            keys = halves(dot3((split[0][:parts], split[1][:parts]), maps[1]))
            values = halves(dot3(maps[2], split, dot_nt))
            lane = lanes((parts, width)) // dim

            def stacked(k):
                return jnp.concatenate(
                    [jnp.where(lane == h, k, jnp.zeros_like(k)) for h in range(heads)],
                    axis=0,
                )

            scores = dot3(tuple(stacked(k) for k in keys), queries, dot_nt)
            probs = []
            factor = dim**-0.5 * LOG2E
            for h in range(heads):
                rows = scores[h * parts : (h + 1) * parts]
                top = jnp.max(rows, axis=0, keepdims=True)
                powers = jnp.exp2((rows - top) * factor)
                probs.append(powers / jnp.sum(powers, axis=0, keepdims=True))
            probs = halves(jnp.concatenate(probs, axis=0))
            row_head = lax.broadcasted_iota(jnp.int32, (width, 2 * parts), 0) // dim
            col_head = lanes((width, 2 * parts)) // parts

            def spaced(v):
                return jnp.concatenate(
                    [
                        jnp.where(row_head == col_head + 2 * t, v, jnp.zeros_like(v))
                        for t in range(heads // 2)
                    ],
                    axis=1,
                )

            mixed = dot3(tuple(spaced(v) for v in values), probs)
            mixed_ref[end_ref[slots + slot]] = spaced(mixed.astype(BF16))

    pieces = []
    for b in range(chunk):
        pieces.append(
            dot(
                mixed_ref[end_ref[slots + step * chunk + b]],
                shares_ref[0, :, b * height : (b + 1) * height],
            ).astype(BF16)
        )
    for b in range(chunk):
        projected = dot(pieces[b].T, readout_ref[...])
        row = lax.broadcasted_iota(jnp.int32, (height, width), 0)
        result = jnp.where(
            row < tally_ref[step * chunk + b], x_ref[b].astype(F32) + projected, 0.0
        )
        out_ref[b] = result.astype(BF16)


def whole(array):
    rank = array.ndim
    return pl.BlockSpec(array.shape, lambda *_: (0,) * rank)


def on_device(
    axes,
    vertex_values,
    label,
    tally,
    gain,
    embedding_matrix,
    partition_input_matrix,
    partition_score_matrix,
    sharpness,
    maps,
    readout_matrix,
):
    slots, height, width = vertex_values.shape
    heads = sharpness.shape[0]
    dim = width // heads
    parts = partition_score_matrix.shape[1]
    steps = slots // CHUNK
    wide = width + 128
    points = CHUNK * height
    gain = gain.reshape(1, width)
    x_spec = pl.BlockSpec((CHUNK, height, width), lambda i, *_: (i, 0, 0))
    shares_spec = pl.BlockSpec((1, heads * parts, points), lambda i, *_: (i, 0, 0))
    shares, sums, ends, end = pl.pallas_call(
        functools.partial(gather_kernel, heads),
        grid_spec=pltpu.PrefetchScalarGridSpec(
            num_scalar_prefetch=2,
            grid=(steps,),
            in_specs=[
                x_spec,
                whole(gain),
                whole(embedding_matrix),
                whole(partition_input_matrix),
                whole(partition_score_matrix),
                pl.BlockSpec(memory_space=pltpu.SMEM),
            ],
            out_specs=[
                shares_spec,
                pl.BlockSpec((CHUNK, parts, wide), lambda i, *_: (i, 0, 0)),
                pl.BlockSpec((2, parts, wide), lambda *_: (0, 0, 0)),
                pl.BlockSpec(memory_space=pltpu.SMEM),
            ],
            scratch_shapes=[
                pltpu.VMEM((parts, wide), F32),
                pltpu.VMEM((width, width), BF16),
                pltpu.VMEM((heads * parts, width), BF16),
            ],
        ),
        out_shape=[
            jax.ShapeDtypeStruct((steps, heads * parts, points), BF16),
            jax.ShapeDtypeStruct((slots, parts, wide), F32),
            jax.ShapeDtypeStruct((2, parts, wide), F32),
            jax.ShapeDtypeStruct((2 * slots + 1,), jnp.int32),
        ],
        name="gather",
    )(
        label,
        tally,
        vertex_values,
        gain,
        embedding_matrix,
        partition_input_matrix,
        partition_score_matrix,
        sharpness,
    )

    rounds = sum(size.bit_length() - 1 for _, size in axes)
    packet = (rounds, 2, parts + heads + 8, width)
    totals = pl.pallas_call(
        functools.partial(exchange_kernel, axes, heads),
        out_shape=jax.ShapeDtypeStruct((2, parts, wide), F32),
        in_specs=[
            pl.BlockSpec(memory_space=pltpu.SMEM),
            pl.BlockSpec(memory_space=pltpu.SMEM),
            pl.BlockSpec(memory_space=pltpu.VMEM),
        ],
        out_specs=pl.BlockSpec(memory_space=pltpu.VMEM),
        scratch_shapes=[
            pltpu.VMEM(packet, BF16),
            pltpu.VMEM(packet, BF16),
            pltpu.SemaphoreType.DMA((rounds,)),
            pltpu.SemaphoreType.DMA((rounds,)),
        ],
        compiler_params=pltpu.CompilerParams(collective_id=0, has_side_effects=True),
        name="exchange",
    )(label, end, ends)

    def sums_spec(b):
        return pl.BlockSpec(
            (1, parts, wide), lambda i, l, t, e: (e[i * CHUNK + b], 0, 0)
        )

    return pl.pallas_call(
        functools.partial(spread_kernel, heads),
        grid_spec=pltpu.PrefetchScalarGridSpec(
            num_scalar_prefetch=3,
            grid=(steps,),
            in_specs=[x_spec, shares_spec]
            + [sums_spec(b) for b in range(CHUNK)]
            + [
                whole(totals),
                whole(maps),
                whole(readout_matrix),
            ],
            out_specs=x_spec,
            scratch_shapes=[
                pltpu.VMEM((CHUNK, width, heads * parts), BF16),
                pltpu.VMEM((3, 2, width, width), BF16),
            ],
        ),
        out_shape=jax.ShapeDtypeStruct(vertex_values.shape, BF16),
        name="spread",
    )(
        label,
        tally,
        end,
        vertex_values,
        shares,
        *([sums] * CHUNK),
        totals,
        maps,
        readout_matrix,
    )


def solution(mesh):
    axes = tuple((name, mesh.shape[name]) for name in mesh.axis_names)
    split = P(mesh.axis_names)
    points = P(mesh.axis_names, None, None)
    return jax.shard_map(
        functools.partial(on_device, axes),
        mesh=mesh,
        in_specs=(points, split, split) + (P(),) * 7,
        out_specs=points,
        check_vma=False,
    )
```

profile of v0, /device:TPU:2, one launch (start us, length us, event | category | flops | bytes accessed | tf_op | source)
XLA Modules:
  0.0 76.5 jit_solution(10503146214845912300)
XLA Ops:
  0.0 26.9 %gather.1 = (bf16[16,512,512]{2,1,0:T(8,128)(2,1)}, f32[64,64,384]{2,1,0:T(8,128)}, f32[2,64,384]{2,1,0:T(8,128)}, s32[129]{0:T(256)}) custom-call(s32[64]{0:T(128)} %label_ref.5, s32[64]{0:T(128)} %tally_ref.3, bf16[64,128,256]{2,1,0:T(8,128)(2,1)} %x_ref.3, f32[1,256]{1,0:T(1,128)} %bitcast.1, bf16[256,256]{1,0:T(8,128)(2,1)} %embed_ref.1, ...), custom_call_target="tpu_custom_call" | custom-call | tf_op jit(solution)/shard_map/gather/pallas_call | solution.py:406
  26.9 21.8 %exchange.1.refs_4_ = f32[2,64,384]{2,1,0:T(8,128)} custom-call(s32[64]{0:T(128)} %label_ref.5, s32[129]{0:T(256)} %get-tuple-element.9.end_ref, f32[2,64,384]{2,1,0:T(8,128)} %get-tuple-element.12.ends_ref), custom_call_target="tpu_custom_call" | custom-call | tf_op jit(solution)/shard_map/exchange/pallas_call | solution.py:451
  48.7 27.9 %spread.1 = bf16[64,128,256]{2,1,0:T(8,128)(2,1)} custom-call(s32[64]{0:T(128)} %label_ref.5, s32[64]{0:T(128)} %tally_ref.3, s32[129]{0:T(256)} %get-tuple-element.9.end_ref, bf16[64,128,256]{2,1,0:T(8,128)(2,1)} %x_ref.3, bf16[16,512,512]{2,1,0:T(8,128)(2,1)} %get-tuple-element.10.shares_ref, ...), custom_call_target="tpu_custom_call" | custom-call | tf_op jit(solution)/shard_map/spread/pallas_call | solution.py:475
where the time goes:
time: 77.7 us; the launch traced here: 76.5 us
  Pallas kernels  76.5 us (98%)
    pallas_call x1, Pallas kernels, on_device(): pl.pallas_call(functools.partial(spread_kernel, heads), grid_spec=pltpu.P...  27.9 us
    pallas_call x1, Pallas kernels, on_device(): pl.pallas_call(functools.partial(gather_kernel, heads), grid_spec=pltpu.P...  26.9 us
    pallas_call x1, Pallas kernels, on_device(): pl.pallas_call(functools.partial(exchange_kernel, axes, heads), out_shape...  21.8 us

commit v1 on v0

--- a/solution.py
+++ b/solution.py
@@ -124,7 +124,7 @@
         sharp = LOG2E / jnp.full((1, points), sharp_ref[h], F32)
         powers = jnp.exp2((rows - top) * sharp)
         scale = living / jnp.sum(powers, axis=0, keepdims=True)
-        shares_ref[0, h * parts : (h + 1) * parts, :] = (powers * scale).astype(BF16)
+        shares_ref[step, h * parts : (h + 1) * parts, :] = (powers * scale).astype(BF16)
 
     ones = jnp.ones((height, 128), BF16)
     share_lane = lanes((parts, half)) // dim
@@ -145,7 +145,7 @@
             )
             got = dot(
                 shares_ref[
-                    0,
+                    step,
                     g * group * parts : (g + 1) * group * parts,
                     b * height : (b + 1) * height,
                 ],
@@ -325,7 +325,7 @@
             maps = [(map_ref[i, 0], map_ref[i, 1]) for i in range(3)]
             queries = halves(dot3(split, maps[0]))
             keys = halves(dot3((split[0][:parts], split[1][:parts]), maps[1]))
-            values = halves(dot3(maps[2], split, dot_nt))
+            values = dot3(maps[2], split, dot_nt).astype(BF16)
             lane = lanes((parts, width)) // dim
 
             def stacked(k):
@@ -342,7 +342,7 @@
                 top = jnp.max(rows, axis=0, keepdims=True)
                 powers = jnp.exp2((rows - top) * factor)
                 probs.append(powers / jnp.sum(powers, axis=0, keepdims=True))
-            probs = halves(jnp.concatenate(probs, axis=0))
+            probs = jnp.concatenate(probs, axis=0).astype(BF16)
             row_head = lax.broadcasted_iota(jnp.int32, (width, 2 * parts), 0) // dim
             col_head = lanes((width, 2 * parts)) // parts
 
@@ -355,7 +355,7 @@
                     axis=1,
                 )
 
-            mixed = dot3(tuple(spaced(v) for v in values), probs)
+            mixed = dot(spaced(values), probs)
             mixed_ref[end_ref[slots + slot]] = spaced(mixed.astype(BF16))
 
     pieces = []
@@ -363,7 +363,7 @@
         pieces.append(
             dot(
                 mixed_ref[end_ref[slots + step * chunk + b]],
-                shares_ref[0, :, b * height : (b + 1) * height],
+                shares_ref[step, :, b * height : (b + 1) * height],
             ).astype(BF16)
         )
     for b in range(chunk):
@@ -402,7 +402,7 @@
     points = CHUNK * height
     gain = gain.reshape(1, width)
     x_spec = pl.BlockSpec((CHUNK, height, width), lambda i, *_: (i, 0, 0))
-    shares_spec = pl.BlockSpec((1, heads * parts, points), lambda i, *_: (i, 0, 0))
+    shares_spec = pl.BlockSpec(memory_space=pltpu.VMEM)
     shares, sums, ends, end = pl.pallas_call(
         functools.partial(gather_kernel, heads),
         grid_spec=pltpu.PrefetchScalarGridSpec(
@@ -429,11 +429,12 @@
             ],
         ),
         out_shape=[
-            jax.ShapeDtypeStruct((steps, heads * parts, points), BF16),
+            pltpu.VMEM((steps, heads * parts, points), BF16),
             jax.ShapeDtypeStruct((slots, parts, wide), F32),
             jax.ShapeDtypeStruct((2, parts, wide), F32),
             jax.ShapeDtypeStruct((2 * slots + 1,), jnp.int32),
         ],
+        compiler_params=pltpu.CompilerParams(vmem_limit_bytes=47 << 20),
         name="gather",
     )(
         label,
@@ -463,7 +464,9 @@
             pltpu.SemaphoreType.DMA((rounds,)),
             pltpu.SemaphoreType.DMA((rounds,)),
         ],
-        compiler_params=pltpu.CompilerParams(collective_id=0, has_side_effects=True),
+        compiler_params=pltpu.CompilerParams(
+            collective_id=0, has_side_effects=True, vmem_limit_bytes=8 << 20
+        ),
         name="exchange",
     )(label, end, ends)
 
@@ -491,6 +494,7 @@
             ],
         ),
         out_shape=jax.ShapeDtypeStruct(vertex_values.shape, BF16),
+        compiler_params=pltpu.CompilerParams(vmem_limit_bytes=47 << 20),
         name="spread",
     )(
         label,

time: 77.7 us -> 85.5 us (1.10)
  local copies, waits for them, and re-layouts: 0 us -> 9.12 us
  Pallas kernels: 76.5 us -> 75.4 us
    unnamed x0 -> x20, local copies, waits for them, and re-layouts: none -> 9.12 us
    pallas_call x1, Pallas kernels: 21.8 us -> 20.7 us  [on_device(): pl.pallas_call(functools.partial(exchange_kernel, axes, heads), out_shape...]
where the time goes in v1:
time: 85.5 us; the launch traced here: 84.5 us
  Pallas kernels  75.4 us (88%)
  local copies, waits for them, and re-layouts  9.12 us (11%)
    pallas_call x1, Pallas kernels, on_device(): pl.pallas_call(functools.partial(spread_kernel, heads), grid_spec=pltpu.P...  27.5 us
    pallas_call x1, Pallas kernels, on_device(): pl.pallas_call(functools.partial(gather_kernel, heads), grid_spec=pltpu.P...  27.1 us
    pallas_call x1, Pallas kernels, on_device(): pl.pallas_call(functools.partial(exchange_kernel, axes, heads), out_shape...  20.7 us
    unnamed x20, local copies, waits for them, and re-layouts  9.12 us

profile of v1, /device:TPU:2, one launch (start us, length us, event | category | flops | bytes accessed | tf_op | source)
XLA Modules:
  0.0 84.5 jit_solution(8845960895233536109)
XLA Ops:
  0.0 0.0 copy-start
  0.0 27.1 %gather.1 = (bf16[16,512,512]{2,1,0:T(8,128)(2,1)S(1)}, f32[64,64,384]{2,1,0:T(8,128)}, f32[2,64,384]{2,1,0:T(8,128)}, s32[129]{0:T(256)}) custom-call(s32[64]{0:T(128)} %label_ref.5, s32[64]{0:T(128)} %tally_ref.3, bf16[64,128,256]{2,1,0:T(8,128)(2,1)} %x_ref.3, f32[1,256]{1,0:T(1,128)} %bitcast.1, bf16[256,256]{1,0:T(8,128)(2,1)} %embed_ref.1, ...), custom_call_target="tpu_custom_call" | custom-call | tf_op jit(solution)/shard_map/gather/pallas_call | solution.py:406
  27.1 0.0 copy-start.1
  27.2 3.2 %copy-done.1 = bf16[16,512,512]{2,1,0:T(8,128)(2,1)} copy-done((bf16[16,512,512]{2,1,0:T(8,128)(2,1)}, bf16[16,512,512]{2,1,0:T(8,128)(2,1)S(1)}, u32[]{:S(2)}) %copy-start.1) | copy-done | bytes 8388632
  30.4 0.0 copy-start.2
  30.4 0.9 %copy-done.2 = f32[2,64,384]{2,1,0:T(8,128)S(1)} copy-done((f32[2,64,384]{2,1,0:T(8,128)S(1)}, f32[2,64,384]{2,1,0:T(8,128)}, u32[]{:S(2)}) %copy-start.2) | copy-done | bytes 196632
  31.3 0.0 copy-start.5
  31.3 0.7 copy-done.5
  32.0 0.0 copy-start.7
  32.0 0.7 copy-done.7
  32.6 20.7 %exchange.1.refs_4_ = f32[2,64,384]{2,1,0:T(8,128)S(1)} custom-call(s32[64]{0:T(128)S(1)} %copy-done.5, s32[129]{0:T(256)S(1)} %copy-done.7, f32[2,64,384]{2,1,0:T(8,128)S(1)} %copy-done.2), custom_call_target="tpu_custom_call" | custom-call | tf_op jit(solution)/shard_map/exchange/pallas_call | solution.py:452
  53.3 0.0 copy-done
  53.3 0.0 copy-start.3
  53.3 0.9 %copy-done.3 = bf16[256,256]{1,0:T(8,128)(2,1)S(1)} copy-done((bf16[256,256]{1,0:T(8,128)(2,1)S(1)}, bf16[256,256]{1,0:T(8,128)(2,1)}, u32[]{:S(2)}) %copy-start.3) | copy-done | bytes 131096
  54.2 0.0 copy-start.4
  54.2 0.8 copy-done.4
  55.0 0.0 copy-start.6
  55.0 0.7 copy-done.6
  55.7 0.0 copy-start.8
  55.7 0.7 copy-done.8
  56.3 0.0 copy-start.9
  56.3 0.7 copy-done.9
  57.0 27.5 %spread.1 = bf16[64,128,256]{2,1,0:T(8,128)(2,1)} custom-call(s32[64]{0:T(128)S(1)} %copy-done.6, s32[64]{0:T(128)S(1)} %copy-done.9, s32[129]{0:T(256)S(1)} %copy-done.8, bf16[64,128,256]{2,1,0:T(8,128)(2,1)S(1)} %copy-done, bf16[16,512,512]{2,1,0:T(8,128)(2,1)} %copy-done.1, f32[64,64,384]{2,1,0:T(8,128)} %get-tuple-element.11.refs_0_.refs_1_.refs_2_.refs_3_, ...), custom_call_target="tpu_custom_call" | custom-call | tf_op jit(solution)/shard_map/spread/pallas_call | solution.py:478
Async XLA Ops:
  0.0 53.3 %copy-start = (bf16[64,128,256]{2,1,0:T(8,128)(2,1)S(1)}, bf16[64,128,256]{2,1,0:T(8,128)(2,1)}, u32[]{:S(2)}) copy-start(bf16[64,128,256]{2,1,0:T(8,128)(2,1)} %x_ref.3) | copy-start | bytes 12582916
  27.1 3.2 %copy-start.1 = (bf16[16,512,512]{2,1,0:T(8,128)(2,1)}, bf16[16,512,512]{2,1,0:T(8,128)(2,1)S(1)}, u32[]{:S(2)}) copy-start(bf16[16,512,512]{2,1,0:T(8,128)(2,1)S(1)} %get-tuple-element.10.shares_ref) | copy-start | bytes 25165828
  30.4 0.9 %copy-start.2 = (f32[2,64,384]{2,1,0:T(8,128)S(1)}, f32[2,64,384]{2,1,0:T(8,128)}, u32[]{:S(2)}) copy-start(f32[2,64,384]{2,1,0:T(8,128)} %get-tuple-element.12.ends_ref) | copy-start | bytes 589828
  31.3 0.7 copy-start.5
  32.0 0.7 copy-start.7
  53.3 0.9 %copy-start.3 = (bf16[256,256]{1,0:T(8,128)(2,1)S(1)}, bf16[256,256]{1,0:T(8,128)(2,1)}, u32[]{:S(2)}) copy-start(bf16[256,256]{1,0:T(8,128)(2,1)} %refs_6_.1) | copy-start | bytes 393220
  54.2 0.8 copy-start.4
  55.0 0.7 copy-start.6
  55.7 0.7 copy-start.8
  56.3 0.7 copy-start.9

commit v2 on v0

--- a/solution.py
+++ b/solution.py
@@ -9,7 +9,7 @@
 from jax.sharding import PartitionSpec as P
 
 MESHES = 64
-CHUNK = 4
+CHUNK = 8
 MESH_ID = pl.DeviceIdType.MESH
 NT = (((1,), (1,)), ((), ()))
 F32 = jnp.float32
@@ -101,66 +101,70 @@
             0, slots, note, (jnp.int32(slots - 1), jnp.int32(-1), jnp.int32(0))
         )[1]
 
-    x = x_ref[...].reshape(points, width).astype(F32)
-    centre = x - jnp.mean(x, axis=1, keepdims=True)
-    var = jnp.mean(centre * centre, axis=1, keepdims=True)
-    normed = (centre * lax.rsqrt(var + 1e-05) * gain_ref[...]).astype(BF16)
-    features = dot(normed, embed_ref[...]).astype(BF16)
-    middles = dot_nt(inputs_t_ref[...], normed).astype(BF16)
+    part_blocks = chunk // 2
+    part_points = part_blocks * height
     lane = lanes((1, height))
-    living = jnp.concatenate(
-        [
-            (lane < tally_ref[step * chunk + b]).astype(F32)
-            for b in range(chunk)
-        ],
-        axis=1,
-    )
-    for h in range(heads):
-        rows = dot(
-            score_t_ref[h * parts : (h + 1) * parts, h // group * half : (h // group + 1) * half],
-            middles[h // group * half : (h // group + 1) * half],
-        )
-        top = jnp.max(rows, axis=0, keepdims=True)
-        sharp = LOG2E / jnp.full((1, points), sharp_ref[h], F32)
-        powers = jnp.exp2((rows - top) * sharp)
-        scale = living / jnp.sum(powers, axis=0, keepdims=True)
-        shares_ref[0, h * parts : (h + 1) * parts, :] = (powers * scale).astype(BF16)
-
     ones = jnp.ones((height, 128), BF16)
     share_lane = lanes((parts, half)) // dim
     total_lane = lanes((parts, 128))
     running = running_ref[...]
+    features = []
+    for s in range(2):
+        x = x_ref[s * part_blocks : (s + 1) * part_blocks]
+        x = x.reshape(part_points, width).astype(F32)
+        centre = x - jnp.mean(x, axis=1, keepdims=True)
+        var = jnp.mean(centre * centre, axis=1, keepdims=True)
+        normed = (centre * lax.rsqrt(var + 1e-05) * gain_ref[...]).astype(BF16)
+        features.append(dot(normed, embed_ref[...]).astype(BF16))
+        middles = dot_nt(inputs_t_ref[...], normed).astype(BF16)
+        living = jnp.concatenate(
+            [
+                (lane < tally_ref[step * chunk + s * part_blocks + b]).astype(F32)
+                for b in range(part_blocks)
+            ],
+            axis=1,
+        )
+        for h in range(heads):
+            rows = dot(
+                score_t_ref[h * parts : (h + 1) * parts, h // group * half : (h // group + 1) * half],
+                middles[h // group * half : (h // group + 1) * half],
+            )
+            top = jnp.max(rows, axis=0, keepdims=True)
+            sharp = LOG2E / jnp.full((1, part_points), sharp_ref[h], F32)
+            powers = jnp.exp2((rows - top) * sharp)
+            scale = living / jnp.sum(powers, axis=0, keepdims=True)
+            shares_ref[
+                0, h * parts : (h + 1) * parts, s * part_points : (s + 1) * part_points
+            ] = (powers * scale).astype(BF16)
+
     for b in range(chunk):
         slot = step * chunk + b
         same = label_ref[slot] == label_ref[jnp.maximum(slot - 1, 0)]
+        row = b % part_blocks * height
+        mine = features[b // part_blocks]
         pieces = []
         totals = None
         for g in range(2):
             right = jnp.concatenate(
-                [
-                    features[b * height : (b + 1) * height, g * half : (g + 1) * half],
-                    ones,
-                ],
-                axis=1,
+                [mine[row : row + height, g * half : (g + 1) * half], ones], axis=1
             )
-            got = dot(
-                shares_ref[
-                    0,
-                    g * group * parts : (g + 1) * group * parts,
-                    b * height : (b + 1) * height,
-                ],
-                right,
-            )
-            piece = got[:parts, :half]
+            piece = None
             for i in range(group):
-                mine = got[i * parts : (i + 1) * parts]
-                piece = jnp.where(share_lane == i, mine[:, :half], piece)
+                h = g * group + i
+                got = dot(
+                    shares_ref[
+                        0, h * parts : (h + 1) * parts, b * height : (b + 1) * height
+                    ],
+                    right,
+                )
+                if piece is None:
+                    piece = got[:, :half]
+                else:
+                    piece = jnp.where(share_lane == i, got[:, :half], piece)
                 if totals is None:
-                    totals = mine[:, half:]
+                    totals = got[:, half:]
                 else:
-                    totals = jnp.where(
-                        total_lane == g * group + i, mine[:, half:], totals
-                    )
+                    totals = jnp.where(total_lane == h, got[:, half:], totals)
             pieces.append(piece)
         running = jnp.where(same, running, 0.0) + jnp.concatenate(
             pieces + [totals], axis=1
@@ -187,12 +191,15 @@
     parts = out_ref.shape[1]
     width = out_ref.shape[2] - 128
     partners = []
+    uppers = []
     for name, size in reversed(axes):
         bit = 1
         while bit < size:
             at = {n: lax.axis_index(n) for n, _ in axes}
             here = at[name]
-            at[name] = here + bit - 2 * bit * (here // bit % 2)
+            upper = here // bit % 2
+            uppers.append(upper)
+            at[name] = here + bit - 2 * bit * upper
             partners.append(tuple(at[n] for n, _ in axes))
             bit *= 2
     barrier = pltpu.get_barrier_semaphore()
@@ -223,9 +230,10 @@
     put(0, 1, last, last_id)
     pl.semaphore_wait(barrier, len(partners))
     for i, partner in enumerate(partners):
+        final = 0 < i == len(partners) - 1
         copy = pltpu.make_async_remote_copy(
-            src_ref=sent.at[i],
-            dst_ref=held.at[i],
+            src_ref=sent.at[i, 0] if final else sent.at[i],
+            dst_ref=held.at[i, 0] if final else held.at[i],
             send_sem=send_sem.at[i],
             recv_sem=recv_sem.at[i],
             device_id=partner,
@@ -233,9 +241,9 @@
         )
         copy.start()
         copy.wait()
-        other_first, other_first_id = load(i, 0)
-        other_last, other_last_id = load(i, 1)
         if i < len(partners) - 1:
+            other_first, other_first_id = load(i, 0)
+            other_last, other_last_id = load(i, 1)
             new_first_id = jnp.minimum(group_first_id, other_first_id)
             new_last_id = jnp.maximum(group_last_id, other_last_id)
             group_first = jnp.where(
@@ -245,11 +253,22 @@
                 (group_last_id == new_last_id)[None], group_last, 0.0
             ) + jnp.where((other_last_id == new_last_id)[None], other_last, 0.0)
             group_first_id, group_last_id = new_first_id, new_last_id
-            put(i + 1, 0, group_first, group_first_id)
-            put(i + 1, 1, group_last, group_last_id)
+            if i + 2 < len(partners):
+                put(i + 1, 0, group_first, group_first_id)
+                put(i + 1, 1, group_last, group_last_id)
+            else:
+                upper = uppers[i + 1] == 1
+                put(
+                    i + 1,
+                    0,
+                    jnp.where(upper, group_first, group_last),
+                    jnp.where(upper, group_first_id, group_last_id),
+                )
 
     def found(i, own_id):
         other_first, other_first_id = load(i, 0)
+        if 0 < i == len(partners) - 1:
+            return jnp.where((own_id == other_first_id)[None], other_first, 0.0)
         other_last, other_last_id = load(i, 1)
         return jnp.where(
             (own_id == other_first_id)[None],
@@ -325,7 +344,7 @@
             maps = [(map_ref[i, 0], map_ref[i, 1]) for i in range(3)]
             queries = halves(dot3(split, maps[0]))
             keys = halves(dot3((split[0][:parts], split[1][:parts]), maps[1]))
-            values = halves(dot3(maps[2], split, dot_nt))
+            values = dot3(maps[2], split, dot_nt).astype(BF16)
             lane = lanes((parts, width)) // dim
 
             def stacked(k):
@@ -342,7 +361,7 @@
                 top = jnp.max(rows, axis=0, keepdims=True)
                 powers = jnp.exp2((rows - top) * factor)
                 probs.append(powers / jnp.sum(powers, axis=0, keepdims=True))
-            probs = halves(jnp.concatenate(probs, axis=0))
+            probs = jnp.concatenate(probs, axis=0).astype(BF16)
             row_head = lax.broadcasted_iota(jnp.int32, (width, 2 * parts), 0) // dim
             col_head = lanes((width, 2 * parts)) // parts
 
@@ -355,7 +374,7 @@
                     axis=1,
                 )
 
-            mixed = dot3(tuple(spaced(v) for v in values), probs)
+            mixed = dot(spaced(values), probs)
             mixed_ref[end_ref[slots + slot]] = spaced(mixed.astype(BF16))
 
     pieces = []

time: 77.7 us -> 65.7 us (0.85)
  Pallas kernels: 76.5 us -> 64.9 us
    pallas_call x1, Pallas kernels: 27.9 us -> 21 us  [on_device(): pl.pallas_call(functools.partial(spread_kernel, heads), grid_spec=pltpu.P...]
    pallas_call x1, Pallas kernels: 26.9 us -> 23 us  [on_device(): pl.pallas_call(functools.partial(gather_kernel, heads), grid_spec=pltpu.P...]
    pallas_call x1, Pallas kernels: 21.8 us -> 20.9 us  [on_device(): pl.pallas_call(functools.partial(exchange_kernel, axes, heads), out_shape...]
where the time goes in v2:
time: 65.7 us; the launch traced here: 65 us
  Pallas kernels  64.9 us (99%)
    pallas_call x1, Pallas kernels, on_device(): pl.pallas_call(functools.partial(gather_kernel, heads), grid_spec=pltpu.P...  23 us
    pallas_call x1, Pallas kernels, on_device(): pl.pallas_call(functools.partial(spread_kernel, heads), grid_spec=pltpu.P...  21 us
    pallas_call x1, Pallas kernels, on_device(): pl.pallas_call(functools.partial(exchange_kernel, axes, heads), out_shape...  20.9 us

profile of v2, /device:TPU:2, one launch (start us, length us, event | category | flops | bytes accessed | tf_op | source)
XLA Modules:
  0.0 65.0 jit_solution(10072951212030680212)
XLA Ops:
  0.0 23.0 %gather.1 = (bf16[8,512,1024]{2,1,0:T(8,128)(2,1)}, f32[64,64,384]{2,1,0:T(8,128)}, f32[2,64,384]{2,1,0:T(8,128)}, s32[129]{0:T(256)}) custom-call(s32[64]{0:T(128)} %label_ref.5, s32[64]{0:T(128)} %tally_ref.3, bf16[64,128,256]{2,1,0:T(8,128)(2,1)} %x_ref.3, f32[1,256]{1,0:T(1,128)} %bitcast.1, bf16[256,256]{1,0:T(8,128)(2,1)} %embed_ref.1, ...), custom_call_target="tpu_custom_call" | custom-call | tf_op jit(solution)/shard_map/gather/pallas_call | solution.py:425
  23.0 20.9 %exchange.1.refs_8_ = f32[2,64,384]{2,1,0:T(8,128)} custom-call(s32[64]{0:T(128)} %label_ref.5, s32[129]{0:T(256)} %get-tuple-element.9.end_ref, f32[2,64,384]{2,1,0:T(8,128)} %get-tuple-element.12.ends_ref), custom_call_target="tpu_custom_call" | custom-call | tf_op jit(solution)/shard_map/exchange/pallas_call | solution.py:470
  43.9 21.0 %spread.1 = bf16[64,128,256]{2,1,0:T(8,128)(2,1)} custom-call(s32[64]{0:T(128)} %label_ref.5, s32[64]{0:T(128)} %tally_ref.3, s32[129]{0:T(256)} %get-tuple-element.9.end_ref, bf16[64,128,256]{2,1,0:T(8,128)(2,1)} %x_ref.3, bf16[8,512,1024]{2,1,0:T(8,128)(2,1)} %get-tuple-element.10.shares_ref, ...), custom_call_target="tpu_custom_call" | custom-call | tf_op jit(solution)/shard_map/spread/pallas_call | solution.py:494
